TPU v7x, 256 devices: a whole 4x4x8 slice. The times are simulated.
256 devices in a mesh: section: 4 (over x), tm: 64 (over y, z, core).
Axes of the slice: x: 4, y: 4, z: 8, core: 2. Of those that a mesh axis runs over, the one named last changes fastest.
Arguments:
- signal: bfloat16 [4, 32768, 256], P(None, 'tm'), may hold values from -6 to 6
- skip_cot: bfloat16 [4, 32768, 256], P(None, 'tm'), may hold values from -6 to 6
- res_cot: bfloat16 [4, 32768, 256], P(None, 'tm'), may hold values from -6 to 6
- w_tap: bfloat16 [4, 256, 512], P('section'), may hold values from -0.25 to 0.25
- w_now: bfloat16 [4, 256, 512], P('section'), may hold values from -0.25 to 0.25
- w_res: bfloat16 [4, 256, 256], P('section'), may hold values from -0.375 to 0.375
- w_skip: bfloat16 [4, 256, 256], P('section'), may hold values from -0.375 to 0.375
Outputs:
- skip_total: bfloat16 [4, 32768, 256], P(None, 'tm')
- input_grads: bfloat16 [4, 4, 32768, 256], P('section', None, 'tm')
- grad_tap: float32 [4, 256, 512], P('section')
- grad_now: float32 [4, 256, 512], P('section')
- grad_res: float32 [4, 256, 256], P('section')
- grad_skip: float32 [4, 256, 256], P('section')
All inputs are finite; a program needn't handle non-finite values.
Results may differ from a plain program's by a relative error of at most 0.01.
Values may be sent and summed in bfloat16 or wider, within the bound.
A program may use at most 64 MiB of HBM per device.

v0:
```python
import math
import jax
import jax.numpy as jnp
from jax import lax
from jax.sharding import PartitionSpec as P

SPAN = 4


def passed_along(x, axis, by):
    size = lax.axis_size(axis)
    pairs = [(i, i + by) for i in range(size) if 0 <= i + by < size]
    return lax.ppermute(x, axis, pairs)


def flat_dot(left, right):
    result = jnp.dot(left.reshape(-1, left.shape[-1]), right, preferred_element_type=jnp.float32)
    return result.reshape(left.shape[:-1] + (right.shape[-1],))


def rows_spanning(left, right):
    return lax.dot_general(
        left.reshape(-1, left.shape[-1]),
        right.reshape(-1, right.shape[-1]),
        (((0,), (0,)), ((), ())),
        preferred_element_type=jnp.float32,
    )


def tap_rows(values, chosen, delayed):
    result = jnp.zeros_like(values)
    for layer_number, selected in chosen:
        if delayed:
            arrived = passed_along(values, "tm", SPAN << layer_number)
        else:
            arrived = passed_along(values, "tm", -(SPAN << layer_number))
        result = jnp.where(selected, arrived, result)
    return result


def gate_parts(tapped, layer_in, weights):
    pre = flat_dot(tapped, weights[0]) + flat_dot(layer_in, weights[1])
    half_width = pre.shape[-1] // 2
    return (jnp.tanh(pre[..., :half_width]), jax.nn.sigmoid(pre[..., half_width:]))


def layer_forward(layer_in, weights, chosen):
    tapped = tap_rows(layer_in, chosen, True)
    tanh_part, sigmoid_part = gate_parts(tapped, layer_in, weights)
    gated = (tanh_part * sigmoid_part).astype(jnp.bfloat16)
    stream_out = (layer_in.astype(jnp.float32) + flat_dot(gated, weights[2])).astype(jnp.bfloat16)
    return (tapped, stream_out, flat_dot(gated, weights[3]))


def layer_backward(layer_in, tapped, grad_out, skip_grad, weights, chosen):
    tanh_part, sigmoid_part = gate_parts(tapped, layer_in, weights)
    gated = (tanh_part * sigmoid_part).astype(jnp.bfloat16)
    grad_gated = flat_dot(grad_out, weights[2].T) + flat_dot(skip_grad, weights[3].T)
    grad_pre = jnp.concatenate(
        [
            grad_gated * sigmoid_part * (1.0 - tanh_part * tanh_part),
            grad_gated * tanh_part * sigmoid_part * (1.0 - sigmoid_part),
        ],
        axis=-1,
    ).astype(jnp.bfloat16)
    terms = (
        rows_spanning(tapped, grad_pre),
        rows_spanning(layer_in, grad_pre),
        rows_spanning(gated, grad_out),
        rows_spanning(gated, skip_grad),
    )
    back_term = flat_dot(grad_pre, weights[0].T).astype(jnp.bfloat16)
    arrived = tap_rows(back_term, chosen, False)
    grad_in = (
        grad_out.astype(jnp.float32)
        + flat_dot(grad_pre, weights[1].T)
        + arrived.astype(jnp.float32)
    )
    return (grad_in.astype(jnp.bfloat16), terms)


def run_sequences(signal, skip_cot, res_cot, w_tap, w_now, w_res, w_skip, section_index, sections):
    number = signal.shape[0]
    per_section = number // sections
    every_tap, every_now, every_res, skip_outputs_all = (
        lax.all_gather(w_tap, "section", axis=0, tiled=True),
        lax.all_gather(w_now, "section", axis=0, tiled=True),
        lax.all_gather(w_res, "section", axis=0, tiled=True),
        lax.all_gather(w_skip, "section", axis=0, tiled=True),
    )
    anchor = section_index * per_section
    stream = lax.dynamic_slice_in_dim(signal, anchor, per_section, 0)
    skip_grad = lax.dynamic_slice_in_dim(skip_cot, anchor, per_section, 0)
    grad_out = lax.dynamic_slice_in_dim(res_cot, anchor, per_section, 0)
    skip_running_sum = jnp.zeros(skip_grad.shape, jnp.float32)
    saved_in = []
    saved_tap = []
    for layer_number in range(sections):
        weights = (
            every_tap[layer_number],
            every_now[layer_number],
            every_res[layer_number],
            skip_outputs_all[layer_number],
        )
        tapped, stream_out, skip_term = layer_forward(stream, weights, [(layer_number, True)])
        saved_in.append(stream)
        saved_tap.append(tapped)
        skip_running_sum = skip_running_sum + skip_term
        stream = stream_out
    skip_total = lax.all_gather(
        skip_running_sum.astype(jnp.bfloat16), "section", axis=0, tiled=True
    )
    grad_list = [None] * sections
    term_list = [None] * sections
    for layer_number in reversed(range(sections)):
        weights = (
            every_tap[layer_number],
            every_now[layer_number],
            every_res[layer_number],
            skip_outputs_all[layer_number],
        )
        grad_in, terms = layer_backward(
            saved_in[layer_number],
            saved_tap[layer_number],
            grad_out,
            skip_grad,
            weights,
            [(layer_number, True)],
        )
        grad_list[layer_number] = grad_in
        term_list[layer_number] = terms
        grad_out = grad_in
    stacked = jnp.stack(grad_list)
    input_grads = lax.all_to_all(stacked, "section", split_axis=0, concat_axis=1, tiled=True)[0]
    partial_sums = (
        lax.psum_scatter(
            jnp.stack([term[0] for term in term_list]), "section", scatter_dimension=0, tiled=True
        ),
        lax.psum_scatter(
            jnp.stack([term[1] for term in term_list]), "section", scatter_dimension=0, tiled=True
        ),
        lax.psum_scatter(
            jnp.stack([term[2] for term in term_list]), "section", scatter_dimension=0, tiled=True
        ),
        lax.psum_scatter(
            jnp.stack([term[3] for term in term_list]), "section", scatter_dimension=0, tiled=True
        ),
    )
    return (skip_total, input_grads, tuple(partial_sums))


def body(signal, skip_cot, res_cot, w_tap, w_now, w_res, w_skip):
    sections = lax.axis_size("section")
    shards = lax.axis_size("tm")
    section_index = lax.axis_index("section")
    number, seq_rows, channels = signal.shape
    skip_total, input_grads, partial_sums = run_sequences(
        signal, skip_cot, res_cot, w_tap, w_now, w_res, w_skip, section_index, sections
    )
    summed = lax.psum((partial_sums[0], partial_sums[1], partial_sums[2], partial_sums[3]), "tm")
    grad_scale = 1.0 / math.sqrt(number * seq_rows * shards)
    return (
        skip_total,
        input_grads[None],
        summed[0] * grad_scale,
        summed[1] * grad_scale,
        summed[2] * grad_scale,
        summed[3] * grad_scale,
    )


def solution(mesh):
    in_specs = (
        P(None, "tm", None),
        P(None, "tm", None),
        P(None, "tm", None),
        P("section", None, None),
        P("section", None, None),
        P("section", None, None),
        P("section", None, None),
    )
    out_specs = (
        P(None, "tm", None),
        P("section", None, "tm", None),
        P("section", None, None),
        P("section", None, None),
        P("section", None, None),
        P("section", None, None),
    )
    return jax.shard_map(body, mesh=mesh, in_specs=in_specs, out_specs=out_specs, check_vma=False)
```

profile of v0, /device:TPU:2, one launch (start us, length us, event | category | flops | bytes accessed | tf_op | source)
XLA Modules:
  0.0 490.8 jit_solution(7062506059764534918)
XLA Ops:
  9.7 5.2 %collective-permute-start = (bf16[1,512,256]{2,1,0:T(8,128)(2,1)S(1)}, bf16[1,512,256]{2,1,0:T(8,128)(2,1)S(1)}, u32[]{:S(2)}, u32[]{:S(2)}) collective-permute-start(bf16[1,512,256]{2,1,0:T(8,128)(2,1)S(1)} %constant_dynamic-slice_fusion), channel_id=1, source_target_pairs={{0,4},{1,5},{2,6},{3,7},{4,8},{5,9},{6,10},{7,11},{8,12},{9,13},{1... | collective-permute-start | bytes 786440 | tf_op jit(solution)/shard_map/ppermute | solution.py:13
  14.9 14.2 %all_gather.18 = bf16[4,256,256]{2,1,0:T(8,128)(2,1)S(1)} all-gather(bf16[1,256,256]{2,1,0:T(8,128)(2,1)} %param.12), channel_id=1, replica_groups=mesh['section'=4,'tm'=64] {'section'}, dimensions={0}, use_global_device_ids=true | all-gather | bytes 655360 | tf_op jit(solution)/shard_map/all_gather | solution.py:88
  29.1 15.1 %all_gather.17 = bf16[4,256,256]{2,1,0:T(8,128)(2,1)S(1)} all-gather(bf16[1,256,256]{2,1,0:T(8,128)(2,1)} %param.13), channel_id=1, replica_groups=mesh['section'=4,'tm'=64] {'section'}, dimensions={0}, use_global_device_ids=true | all-gather | bytes 655360 | tf_op jit(solution)/shard_map/all_gather | solution.py:89
  44.3 2.2 fusion.63
  48.8 19.7 %all-gather.5.cloned.1.call-done = bf16[4,256,512]{2,1,0:T(8,128)(2,1)} async-done(((bf16[1,256,512]{2,1,0:T(8,128)(2,1)}), bf16[4,256,512]{2,1,0:T(8,128)(2,1)}) %all-gather.5.cloned.1.call-update) | async-done | bytes 1048592 | tf_op jit(solution)/shard_map/all_gather | solution.py:86
  70.5 7.8 %collective-permute-start.1 = (bf16[1,512,256]{2,1,0:T(8,128)(2,1)S(1)}, bf16[1,512,256]{2,1,0:T(8,128)(2,1)S(1)}, u32[]{:S(2)}, u32[]{:S(2)}) collective-permute-start(bf16[1,512,256]{2,1,0:T(8,128)(2,1)S(1)} %fusion.14), channel_id=1, source_target_pairs={{0,8},{1,9},{2,10},{3,11},{4,12},{5,13},{6,14},{7,15},{8,16},{9,17... | collective-permute-start | bytes 786440 | tf_op jit(solution)/shard_map/ppermute | solution.py:13
  78.7 5.4 %collective-permute-done.1 = bf16[1,512,256]{2,1,0:T(8,128)(2,1)S(1)} collective-permute-done((bf16[1,512,256]{2,1,0:T(8,128)(2,1)S(1)}, bf16[1,512,256]{2,1,0:T(8,128)(2,1)S(1)}, u32[]{:S(2)}, u32[]{:S(2)}) %collective-permute-start.1) | collective-permute-done | bytes 262176 | tf_op jit(solution)/shard_map/ppermute | solution.py:13
  86.3 5.7 %collective-permute-start.2 = (bf16[1,512,256]{2,1,0:T(8,128)(2,1)S(1)}, bf16[1,512,256]{2,1,0:T(8,128)(2,1)}, u32[]{:S(2)}, u32[]{:S(2)}) collective-permute-start(bf16[1,512,256]{2,1,0:T(8,128)(2,1)S(1)} %fusion.13), channel_id=1, source_target_pairs={{0,16},{1,17},{2,18},{3,19},{4,20},{5,21},{6,22},{7,23},{8,24},{9,... | collective-permute-start | bytes 786440 | tf_op jit(solution)/shard_map/ppermute | solution.py:13
  92.3 2.8 collective-permute-done.2
  98.2 6.2 %collective-permute-start.3 = (bf16[1,512,256]{2,1,0:T(8,128)(2,1)S(1)}, bf16[1,512,256]{2,1,0:T(8,128)(2,1)S(1)}, u32[]{:S(2)}, u32[]{:S(2)}) collective-permute-start(bf16[1,512,256]{2,1,0:T(8,128)(2,1)S(1)} %fusion.12), channel_id=1, source_target_pairs={{0,32},{1,33},{2,34},{3,35},{4,36},{5,37},{6,38},{7,39},{8,40},{9,... | collective-permute-start | bytes 786440 | tf_op jit(solution)/shard_map/ppermute | solution.py:13
  104.7 3.5 collective-permute-done.3
  112.9 7.4 %collective-permute-done.4 = bf16[1,512,256]{2,1,0:T(8,128)(2,1)} collective-permute-done((bf16[1,512,256]{2,1,0:T(8,128)(2,1)}, bf16[1,512,256]{2,1,0:T(8,128)(2,1)}, u32[]{:S(2)}, u32[]{:S(2)}) %collective-permute-start.4) | collective-permute-done | bytes 262176 | tf_op jit(solution)/shard_map/ppermute | solution.py:13
  120.3 1.6 add_convert_fusion.3
  121.9 1.9 fusion.38
  127.2 5.5 %collective-permute-done.5 = bf16[1,512,256]{2,1,0:T(8,128)(2,1)S(1)} collective-permute-done((bf16[1,512,256]{2,1,0:T(8,128)(2,1)S(1)}, bf16[1,512,256]{2,1,0:T(8,128)(2,1)S(1)}, u32[]{:S(2)}, u32[]{:S(2)}) %collective-permute-start.5) | collective-permute-done | bytes 262176 | tf_op jit(solution)/shard_map/ppermute | solution.py:13
  136.6 10.4 %collective-permute-done.6 = bf16[1,512,256]{2,1,0:T(8,128)(2,1)S(1)} collective-permute-done((bf16[1,512,256]{2,1,0:T(8,128)(2,1)S(1)}, bf16[1,512,256]{2,1,0:T(8,128)(2,1)S(1)}, u32[]{:S(2)}, u32[]{:S(2)}) %collective-permute-start.6) | collective-permute-done | bytes 262176 | tf_op jit(solution)/shard_map/ppermute | solution.py:13
  167.1 14.1 %collective-permute-done.7 = bf16[1,512,256]{2,1,0:T(8,128)(2,1)S(1)} collective-permute-done((bf16[1,512,256]{2,1,0:T(8,128)(2,1)S(1)}, bf16[1,512,256]{2,1,0:T(8,128)(2,1)S(1)}, u32[]{:S(2)}, u32[]{:S(2)}) %collective-permute-start.7) | collective-permute-done | bytes 262176 | tf_op jit(solution)/shard_map/ppermute | solution.py:13
  183.7 6.6 %all-to-all-start = ((bf16[4,1,512,256]{3,2,1,0:T(8,128)(2,1)}), bf16[4,1,512,256]{3,2,1,0:T(8,128)(2,1)S(1)}, u32[]{:S(2)}, u32[]{:S(2)}) async-start(bf16[4,1,512,256]{3,2,1,0:T(8,128)(2,1)} %pad_maximum_fusion.2), calls=%async_computation | async-start | bytes 2097152 | tf_op jit(solution)/shard_map/all_to_all | solution.py:134
  190.3 27.4 %reduce-scatter.7.cloned.1.call-done = f32[1,256,512]{2,1,0:T(8,128)} async-done(((f32[4,256,512]{2,1,0:T(8,128)}), f32[1,256,512]{2,1,0:T(8,128)}) %reduce-scatter.7.cloned.1.call-update) | async-done | bytes 524304 | tf_op jit(solution)/shard_map/reduce_scatter | solution.py:139
  217.7 36.6 %reduce-scatter.5.cloned.1.call-done = f32[1,256,512]{2,1,0:T(8,128)} async-done(((f32[4,256,512]{2,1,0:T(8,128)}), f32[1,256,512]{2,1,0:T(8,128)}) %reduce-scatter.5.cloned.1.call-update) | async-done | bytes 524304 | tf_op jit(solution)/shard_map/reduce_scatter | solution.py:136
  254.4 28.9 %all-gather.9.cloned.1.call-done = bf16[2048,256]{1,0:T(8,128)(2,1)} async-done(((bf16[512,256]{1,0:T(8,128)(2,1)}), bf16[2048,256]{1,0:T(8,128)(2,1)}) %all-gather.9.cloned.1.call-update) | async-done | bytes 1048592 | tf_op jit(solution)/shard_map/all_gather | solution.py:110
  283.2 194.7 %all-reduce.3.cloned.1.call-done = (f32[1,256,512]{2,1,0:T(8,128)}, f32[1,256,512]{2,1,0:T(8,128)}, f32[1,256,256]{2,1,0:T(8,128)}, f32[1,256,256]{2,1,0:T(8,128)}) async-done(((f32[1,256,512]{2,1,0:T(8,128)}, f32[1,256,512]{2,1,0:T(8,128)}, f32[1,256,256]{2,1,0:T(8,128)}, f32[1,256,256]{2,1,0:T(8,128)}), (f32[1,256,512]{2,1,0:T(8,128)}, f32[1,256,512]{2,1,0:T(8,128)}, f32[1,256,256]{2,1,0:T(8,128)}, ...) | async-done | bytes 1572880 | tf_op jit(solution)/shard_map/psum | solution.py:160
  477.9 1.9 broadcast_multiply_fusion.2
  479.8 2.3 broadcast_multiply_fusion
  (172 shorter events, 48.8 us)
Async XLA Ops:
  7.2 39.3 %copy-start = (bf16[4,512,256]{2,1,0:T(8,128)(2,1)S(1)}, bf16[4,512,256]{2,1,0:T(8,128)(2,1)}, u32[]{:S(2)}) copy-start(bf16[4,512,256]{2,1,0:T(8,128)(2,1)} %param.8) | copy-start | bytes 3145732
  7.2 40.3 %all-gather.7.cloned.1.call-start = ((), (), s32[]{:S(2)}) async-start(), calls=%async_computation.6 | async-start | bytes 1310720 | tf_op jit(solution)/shard_map/all_gather | solution.py:87
  7.9 60.6 %all-gather.5.cloned.1.call-start = ((), (), s32[]{:S(2)}) async-start(), calls=%async_computation.5 | async-start | bytes 1310720 | tf_op jit(solution)/shard_map/all_gather | solution.py:86
  8.7 181.6 %reduce-scatter.11.cloned.1.call-start = ((), (), s32[]{:S(2)}) async-start(), calls=%async_computation.10 | async-start | bytes 1310720 | tf_op jit(solution)/shard_map/reduce_scatter | solution.py:145
  9.7 39.1 %collective-permute-start = (bf16[1,512,256]{2,1,0:T(8,128)(2,1)S(1)}, bf16[1,512,256]{2,1,0:T(8,128)(2,1)S(1)}, u32[]{:S(2)}, u32[]{:S(2)}) collective-permute-start(bf16[1,512,256]{2,1,0:T(8,128)(2,1)S(1)} %constant_dynamic-slice_fusion), channel_id=1, source_target_pairs={{0,4},{1,5},{2,6},{3,7},{4,8},{5,9},{6,10},{7,11},{8,12},{9,13},{1... | collective-permute-start | bytes 786440 | tf_op jit(solution)/shard_map/ppermute | solution.py:13
  29.1 55.0 %copy-start.11 = (bf16[4,256,256]{2,1,0:T(8,128)(2,1)}, bf16[4,256,256]{2,1,0:T(8,128)(2,1)S(1)}, u32[]{:S(2)}) copy-start(bf16[4,256,256]{2,1,0:T(8,128)(2,1)S(1)} %all_gather.18) | copy-start | bytes 1572868
  48.8 19.7 %copy-start.14 = (bf16[1,512,256]{2,1,0:T(8,128)(2,1)}, bf16[1,512,256]{2,1,0:T(8,128)(2,1)S(1)}, u32[]{:S(2)}) copy-start(bf16[1,512,256]{2,1,0:T(8,128)(2,1)S(1)} %collective-permute-done) | copy-start | bytes 786436
  70.5 13.6 %collective-permute-start.1 = (bf16[1,512,256]{2,1,0:T(8,128)(2,1)S(1)}, bf16[1,512,256]{2,1,0:T(8,128)(2,1)S(1)}, u32[]{:S(2)}, u32[]{:S(2)}) collective-permute-start(bf16[1,512,256]{2,1,0:T(8,128)(2,1)S(1)} %fusion.14), channel_id=1, source_target_pairs={{0,8},{1,9},{2,10},{3,11},{4,12},{5,13},{6,14},{7,15},{8,16},{9,17... | collective-permute-start | bytes 786440 | tf_op jit(solution)/shard_map/ppermute | solution.py:13
  86.3 8.8 %collective-permute-start.2 = (bf16[1,512,256]{2,1,0:T(8,128)(2,1)S(1)}, bf16[1,512,256]{2,1,0:T(8,128)(2,1)}, u32[]{:S(2)}, u32[]{:S(2)}) collective-permute-start(bf16[1,512,256]{2,1,0:T(8,128)(2,1)S(1)} %fusion.13), channel_id=1, source_target_pairs={{0,16},{1,17},{2,18},{3,19},{4,20},{5,21},{6,22},{7,23},{8,24},{9,... | collective-permute-start | bytes 786440 | tf_op jit(solution)/shard_map/ppermute | solution.py:13
  98.2 10.0 %collective-permute-start.3 = (bf16[1,512,256]{2,1,0:T(8,128)(2,1)S(1)}, bf16[1,512,256]{2,1,0:T(8,128)(2,1)S(1)}, u32[]{:S(2)}, u32[]{:S(2)}) collective-permute-start(bf16[1,512,256]{2,1,0:T(8,128)(2,1)S(1)} %fusion.12), channel_id=1, source_target_pairs={{0,32},{1,33},{2,34},{3,35},{4,36},{5,37},{6,38},{7,39},{8,40},{9,... | collective-permute-start | bytes 786440 | tf_op jit(solution)/shard_map/ppermute | solution.py:13
  110.2 10.1 %collective-permute-start.4 = (bf16[1,512,256]{2,1,0:T(8,128)(2,1)}, bf16[1,512,256]{2,1,0:T(8,128)(2,1)}, u32[]{:S(2)}, u32[]{:S(2)}) collective-permute-start(bf16[1,512,256]{2,1,0:T(8,128)(2,1)} %fusion.16), channel_id=1, source_target_pairs={{32,0},{33,1},{34,2},{35,3},{36,4},{37,5},{38,6},{39,7},{40,8},{41... | collective-permute-start | bytes 786440 | tf_op jit(solution)/shard_map/ppermute | solution.py:13
  112.8 77.5 %reduce-scatter.9.cloned.1.call-start = ((), (), s32[]{:S(2)}) async-start(), calls=%async_computation.9 | async-start | bytes 1310720 | tf_op jit(solution)/shard_map/reduce_scatter | solution.py:142
  124.2 8.4 %collective-permute-start.5 = (bf16[1,512,256]{2,1,0:T(8,128)(2,1)S(1)}, bf16[1,512,256]{2,1,0:T(8,128)(2,1)S(1)}, u32[]{:S(2)}, u32[]{:S(2)}) collective-permute-start(bf16[1,512,256]{2,1,0:T(8,128)(2,1)S(1)} %fusion.17), channel_id=1, source_target_pairs={{16,0},{17,1},{18,2},{19,3},{20,4},{21,5},{22,6},{23,7},{24,8},{25... | collective-permute-start | bytes 786440 | tf_op jit(solution)/shard_map/ppermute | solution.py:13
  134.9 12.2 %collective-permute-start.6 = (bf16[1,512,256]{2,1,0:T(8,128)(2,1)S(1)}, bf16[1,512,256]{2,1,0:T(8,128)(2,1)S(1)}, u32[]{:S(2)}, u32[]{:S(2)}) collective-permute-start(bf16[1,512,256]{2,1,0:T(8,128)(2,1)S(1)} %fusion.18), channel_id=1, source_target_pairs={{8,0},{9,1},{10,2},{11,3},{12,4},{13,5},{14,6},{15,7},{16,8},{17,9... | collective-permute-start | bytes 786440 | tf_op jit(solution)/shard_map/ppermute | solution.py:13
  149.2 68.5 %reduce-scatter.7.cloned.1.call-start = ((), (), s32[]{:S(2)}) async-start(), calls=%async_computation.8 | async-start | bytes 2621440 | tf_op jit(solution)/shard_map/reduce_scatter | solution.py:139
  155.9 98.5 %reduce-scatter.5.cloned.1.call-start = ((), (), s32[]{:S(2)}) async-start(), calls=%async_computation.7 | async-start | bytes 2621440 | tf_op jit(solution)/shard_map/reduce_scatter | solution.py:136
  162.5 120.8 %all-gather.9.cloned.1.call-start = ((), (), s32[]{:S(2)}) async-start(), calls=%async_computation.11 | async-start | bytes 1310720 | tf_op jit(solution)/shard_map/all_gather | solution.py:110
  164.4 18.2 %copy-start.39 = (bf16[1,512,256]{2,1,0:T(8,128)(2,1)S(1)}, bf16[1,512,256]{2,1,0:T(8,128)(2,1)}, u32[]{:S(2)}) copy-start(bf16[1,512,256]{2,1,0:T(8,128)(2,1)} %copy-done.38) | copy-start | bytes 786436
  164.4 18.2 %copy-start.41 = (bf16[1,512,256]{2,1,0:T(8,128)(2,1)S(1)}, bf16[1,512,256]{2,1,0:T(8,128)(2,1)}, u32[]{:S(2)}) copy-start(bf16[1,512,256]{2,1,0:T(8,128)(2,1)} %copy-done.40) | copy-start | bytes 786436
  164.4 18.2 %copy-start.44 = (bf16[1,512,256]{2,1,0:T(8,128)(2,1)S(1)}, bf16[1,512,256]{2,1,0:T(8,128)(2,1)}, u32[]{:S(2)}) copy-start(bf16[1,512,256]{2,1,0:T(8,128)(2,1)} %copy-done.42) | copy-start | bytes 786436
  165.8 15.4 %collective-permute-start.7 = (bf16[1,512,256]{2,1,0:T(8,128)(2,1)S(1)}, bf16[1,512,256]{2,1,0:T(8,128)(2,1)S(1)}, u32[]{:S(2)}, u32[]{:S(2)}) collective-permute-start(bf16[1,512,256]{2,1,0:T(8,128)(2,1)S(1)} %fusion.19), channel_id=1, source_target_pairs={{4,0},{5,1},{6,2},{7,3},{8,4},{9,5},{10,6},{11,7},{12,8},{13,9},{1... | collective-permute-start | bytes 786440 | tf_op jit(solution)/shard_map/ppermute | solution.py:13
  183.7 99.5 %all-to-all-start = ((bf16[4,1,512,256]{3,2,1,0:T(8,128)(2,1)}), bf16[4,1,512,256]{3,2,1,0:T(8,128)(2,1)S(1)}, u32[]{:S(2)}, u32[]{:S(2)}) async-start(bf16[4,1,512,256]{3,2,1,0:T(8,128)(2,1)} %pad_maximum_fusion.2), calls=%async_computation | async-start | bytes 2097152 | tf_op jit(solution)/shard_map/all_to_all | solution.py:134
  190.3 287.6 %all-reduce.3.cloned.1.call-start = ((), (), s32[]{:S(2)}) async-start(), calls=%async_computation.12 | async-start | bytes 3145728 | tf_op jit(solution)/shard_map/psum | solution.py:160
  283.2 198.8 %copy-start.35 = (bf16[2048,256]{1,0:T(8,128)(2,1)S(1)}, bf16[2048,256]{1,0:T(8,128)(2,1)}, u32[]{:S(2)}) copy-start(bf16[2048,256]{1,0:T(8,128)(2,1)} %all-gather.9.cloned.1.call-done) | copy-start | bytes 3145732
  (39 other events, 211.1 us)
Sparse Core Ops, SparseCore 0:
  9.8 30.3 all-gather.6
  42.0 26.4 all-gather.4
  113.0 31.7 reduce-scatter.10
  149.3 30.7 reduce-scatter.8
  182.5 35.1 reduce-scatter.6
  220.1 34.1 reduce-scatter.4
  256.7 26.4 all-gather.8
  286.9 190.9 all-reduce.2
where the time goes:
time: 492 us; the launch traced here: 491 us
  waiting for transfers between devices  358 us (73%)
  starting transfers between devices  37.1 us (8%)
  matrix products  35.9 us (7%)
  blocking collectives  29.4 us (6%)
  between operations  15.1 us (3%)
  other arithmetic  11.1 us (2%)
    psum x1, waiting for transfers between devices, body(): lax.psum((partial_sums[0], partial_sums[1], partial_sums[2], partial_sums...  195 us
    ppermute x8, waiting for transfers between devices, passed_along(): return lax.ppermute(x, axis, pairs)  49.1 us
    reduce_scatter x1, waiting for transfers between devices, run_sequences(): lax.psum_scatter(jnp.stack([term[0] for term in term_list]), 'section', s...  36.6 us
    ppermute x8, starting transfers between devices, passed_along(): return lax.ppermute(x, axis, pairs)  30.1 us
    all_gather x1, waiting for transfers between devices, run_sequences(): lax.all_gather(skip_running_sum.astype(jnp.bfloat16), 'section', axis=0,...  28.9 us
    reduce_scatter x1, waiting for transfers between devices, run_sequences(): lax.psum_scatter(jnp.stack([term[1] for term in term_list]), 'section', s...  27.4 us
    dot_general x31, matrix products, flat_dot(): jnp.dot(left.reshape(-1, left.shape[-1]), right, preferred_element_type=j...  25.9 us
    all_gather x1, waiting for transfers between devices, run_sequences(): lax.all_gather(w_tap, 'section', axis=0, tiled=True)  19.7 us
  transfers between devices with their start and end apart: 17, of which 12 were waited for; matrix products, arithmetic and copies ran while one was open for 7% of the time, Pallas kernels for 0%

commit v1 on v0

--- a/solution.py
+++ b/solution.py
@@ -107,9 +107,9 @@
         saved_tap.append(tapped)
         skip_running_sum = skip_running_sum + skip_term
         stream = stream_out
-    skip_total = lax.all_gather(
-        skip_running_sum.astype(jnp.bfloat16), "section", axis=0, tiled=True
-    )
+    block = skip_running_sum.astype(jnp.bfloat16)
+    outgoing = jnp.stack([block] * lax.axis_size("section"))
+    skip_total = jnp.concatenate(lax.all_to_all(outgoing, "section", 0, 0), axis=0)
     grad_list = [None] * sections
     term_list = [None] * sections
     for layer_number in reversed(range(sections)):

time: 492 us -> 467 us (0.949)
  waiting for transfers between devices: 358 us -> 330 us
    all_gather x1 -> x0, waiting for transfers between devices: 28.9 us -> none  [run_sequences(): lax.all_gather(skip_running_sum.astype(jnp.bfloat16), 'section', axis=0,...]
    all_to_all x0 -> x1, starting transfers between devices: none -> 5.21 us  [run_sequences(): lax.all_to_all(outgoing, 'section', 0, 0)]
  transfers between devices with their start and end apart: 17 -> 17, of which waited for: 12 -> 11; matrix products, arithmetic and copies ran while one was open for 7% -> 8% of each run, Pallas kernels for 0% -> 0%
where the time goes in v1:
time: 467 us; the launch traced here: 466 us
  waiting for transfers between devices  330 us (71%)
  starting transfers between devices  39.7 us (9%)
  matrix products  34.2 us (7%)
  blocking collectives  29.4 us (6%)
  between operations  15.1 us (3%)
  other arithmetic  11.2 us (2%)
  local copies, waits for them, and re-layouts  6.23 us (1%)
    psum x1, waiting for transfers between devices, body(): lax.psum((partial_sums[0], partial_sums[1], partial_sums[2], partial_sums...  194 us
    ppermute x8, waiting for transfers between devices, passed_along(): return lax.ppermute(x, axis, pairs)  52.6 us
    reduce_scatter x1, waiting for transfers between devices, run_sequences(): lax.psum_scatter(jnp.stack([term[0] for term in term_list]), 'section', s...  35.1 us
    ppermute x8, starting transfers between devices, passed_along(): return lax.ppermute(x, axis, pairs)  29.3 us
    reduce_scatter x1, waiting for transfers between devices, run_sequences(): lax.psum_scatter(jnp.stack([term[1] for term in term_list]), 'section', s...  26.8 us
    dot_general x31, matrix products, flat_dot(): jnp.dot(left.reshape(-1, left.shape[-1]), right, preferred_element_type=j...  24.2 us
    all_gather x1, waiting for transfers between devices, run_sequences(): lax.all_gather(w_tap, 'section', axis=0, tiled=True)  19.6 us
    all_gather x1, blocking collectives, run_sequences(): lax.all_gather(w_skip, 'section', axis=0, tiled=True)  15.1 us
  transfers between devices with their start and end apart: 17, of which 11 were waited for; matrix products, arithmetic and copies ran while one was open for 8% of the time, Pallas kernels for 0%

profile of v1, /device:TPU:2, one launch (start us, length us, event | category | flops | bytes accessed | tf_op | source)
XLA Modules:
  0.0 465.7 jit_solution(3592351414632953267)
XLA Ops:
  9.7 5.2 %collective-permute-start = (bf16[1,512,256]{2,1,0:T(8,128)(2,1)S(1)}, bf16[1,512,256]{2,1,0:T(8,128)(2,1)S(1)}, u32[]{:S(2)}, u32[]{:S(2)}) collective-permute-start(bf16[1,512,256]{2,1,0:T(8,128)(2,1)S(1)} %constant_dynamic-slice_fusion), channel_id=1, source_target_pairs={{0,4},{1,5},{2,6},{3,7},{4,8},{5,9},{6,10},{7,11},{8,12},{9,13},{1... | collective-permute-start | bytes 786440 | tf_op jit(solution)/shard_map/ppermute | solution.py:13
  14.9 14.2 %all_gather.15 = bf16[4,256,256]{2,1,0:T(8,128)(2,1)S(1)} all-gather(bf16[1,256,256]{2,1,0:T(8,128)(2,1)} %param.12), channel_id=1, replica_groups=mesh['section'=4,'tm'=64] {'section'}, dimensions={0}, use_global_device_ids=true | all-gather | bytes 655360 | tf_op jit(solution)/shard_map/all_gather | solution.py:88
  29.1 15.1 %all_gather.14 = bf16[4,256,256]{2,1,0:T(8,128)(2,1)S(1)} all-gather(bf16[1,256,256]{2,1,0:T(8,128)(2,1)} %param.13), channel_id=1, replica_groups=mesh['section'=4,'tm'=64] {'section'}, dimensions={0}, use_global_device_ids=true | all-gather | bytes 655360 | tf_op jit(solution)/shard_map/all_gather | solution.py:89
  44.3 2.2 fusion.63
  48.8 19.6 %all-gather.3.cloned.1.call-done = bf16[4,256,512]{2,1,0:T(8,128)(2,1)} async-done(((bf16[1,256,512]{2,1,0:T(8,128)(2,1)}), bf16[4,256,512]{2,1,0:T(8,128)(2,1)}) %all-gather.3.cloned.1.call-update) | async-done | bytes 1048592 | tf_op jit(solution)/shard_map/all_gather | solution.py:86
  70.5 7.8 %collective-permute-start.1 = (bf16[1,512,256]{2,1,0:T(8,128)(2,1)S(1)}, bf16[1,512,256]{2,1,0:T(8,128)(2,1)S(1)}, u32[]{:S(2)}, u32[]{:S(2)}) collective-permute-start(bf16[1,512,256]{2,1,0:T(8,128)(2,1)S(1)} %fusion.14), channel_id=1, source_target_pairs={{0,8},{1,9},{2,10},{3,11},{4,12},{5,13},{6,14},{7,15},{8,16},{9,17... | collective-permute-start | bytes 786440 | tf_op jit(solution)/shard_map/ppermute | solution.py:13
  78.7 5.4 %collective-permute-done.1 = bf16[1,512,256]{2,1,0:T(8,128)(2,1)S(1)} collective-permute-done((bf16[1,512,256]{2,1,0:T(8,128)(2,1)S(1)}, bf16[1,512,256]{2,1,0:T(8,128)(2,1)S(1)}, u32[]{:S(2)}, u32[]{:S(2)}) %collective-permute-start.1) | collective-permute-done | bytes 262176 | tf_op jit(solution)/shard_map/ppermute | solution.py:13
  86.3 4.9 %collective-permute-start.2 = (bf16[1,512,256]{2,1,0:T(8,128)(2,1)S(1)}, bf16[1,512,256]{2,1,0:T(8,128)(2,1)S(1)}, u32[]{:S(2)}, u32[]{:S(2)}) collective-permute-start(bf16[1,512,256]{2,1,0:T(8,128)(2,1)S(1)} %fusion.13), channel_id=1, source_target_pairs={{0,16},{1,17},{2,18},{3,19},{4,20},{5,21},{6,22},{7,23},{8,24},{9,... | collective-permute-start | bytes 786440 | tf_op jit(solution)/shard_map/ppermute | solution.py:13
  91.6 3.5 collective-permute-done.2
  98.0 6.1 %collective-permute-start.3 = (bf16[1,512,256]{2,1,0:T(8,128)(2,1)S(1)}, bf16[1,512,256]{2,1,0:T(8,128)(2,1)S(1)}, u32[]{:S(2)}, u32[]{:S(2)}) collective-permute-start(bf16[1,512,256]{2,1,0:T(8,128)(2,1)S(1)} %fusion.12), channel_id=1, source_target_pairs={{0,32},{1,33},{2,34},{3,35},{4,36},{5,37},{6,38},{7,39},{8,40},{9,... | collective-permute-start | bytes 786440 | tf_op jit(solution)/shard_map/ppermute | solution.py:13
  104.4 3.5 collective-permute-done.3
  112.5 7.4 %collective-permute-done.4 = bf16[1,512,256]{2,1,0:T(8,128)(2,1)} collective-permute-done((bf16[1,512,256]{2,1,0:T(8,128)(2,1)}, bf16[1,512,256]{2,1,0:T(8,128)(2,1)}, u32[]{:S(2)}, u32[]{:S(2)}) %collective-permute-start.4) | collective-permute-done | bytes 262176 | tf_op jit(solution)/shard_map/ppermute | solution.py:13
  119.9 1.6 add_convert_fusion.3
  121.5 1.9 fusion.38
  126.8 5.5 %collective-permute-done.5 = bf16[1,512,256]{2,1,0:T(8,128)(2,1)S(1)} collective-permute-done((bf16[1,512,256]{2,1,0:T(8,128)(2,1)S(1)}, bf16[1,512,256]{2,1,0:T(8,128)(2,1)S(1)}, u32[]{:S(2)}, u32[]{:S(2)}) %collective-permute-start.5) | collective-permute-done | bytes 262176 | tf_op jit(solution)/shard_map/ppermute | solution.py:13
  136.3 10.4 %collective-permute-done.6 = bf16[1,512,256]{2,1,0:T(8,128)(2,1)S(1)} collective-permute-done((bf16[1,512,256]{2,1,0:T(8,128)(2,1)S(1)}, bf16[1,512,256]{2,1,0:T(8,128)(2,1)S(1)}, u32[]{:S(2)}, u32[]{:S(2)}) %collective-permute-start.6) | collective-permute-done | bytes 262176 | tf_op jit(solution)/shard_map/ppermute | solution.py:13
  164.5 5.2 %all-to-all-start = ((bf16[4,1,512,256]{3,2,1,0:T(8,128)(2,1)}), bf16[4,1,512,256]{3,2,1,0:T(8,128)(2,1)S(1)}, u32[]{:S(2)}, u32[]{:S(2)}) async-start(bf16[4,1,512,256]{3,2,1,0:T(8,128)(2,1)} %stack.82), calls=%async_computation | async-start | bytes 2097152 | tf_op jit(solution)/shard_map/all_to_all | solution.py:112
  172.4 16.9 %collective-permute-done.7 = bf16[1,512,256]{2,1,0:T(8,128)(2,1)S(1)} collective-permute-done((bf16[1,512,256]{2,1,0:T(8,128)(2,1)S(1)}, bf16[1,512,256]{2,1,0:T(8,128)(2,1)S(1)}, u32[]{:S(2)}, u32[]{:S(2)}) %collective-permute-start.7) | collective-permute-done | bytes 262176 | tf_op jit(solution)/shard_map/ppermute | solution.py:13
  191.7 4.8 %all-to-all-start.1 = ((bf16[4,1,512,256]{3,2,1,0:T(8,128)(2,1)}), bf16[4,1,512,256]{3,2,1,0:T(8,128)(2,1)S(1)}, u32[]{:S(2)}, u32[]{:S(2)}) async-start(bf16[4,1,512,256]{3,2,1,0:T(8,128)(2,1)} %pad_maximum_fusion.2), calls=%async_computation.1 | async-start | bytes 2097152 | tf_op jit(solution)/shard_map/all_to_all | solution.py:134
  196.5 26.8 %reduce-scatter.7.cloned.1.call-done = f32[1,256,512]{2,1,0:T(8,128)} async-done(((f32[4,256,512]{2,1,0:T(8,128)}), f32[1,256,512]{2,1,0:T(8,128)}) %reduce-scatter.7.cloned.1.call-update) | async-done | bytes 524304 | tf_op jit(solution)/shard_map/reduce_scatter | solution.py:139
  223.3 35.1 %reduce-scatter.5.cloned.1.call-done = f32[1,256,512]{2,1,0:T(8,128)} async-done(((f32[4,256,512]{2,1,0:T(8,128)}), f32[1,256,512]{2,1,0:T(8,128)}) %reduce-scatter.5.cloned.1.call-update) | async-done | bytes 524304 | tf_op jit(solution)/shard_map/reduce_scatter | solution.py:136
  258.5 194.2 %all-reduce.3.cloned.1.call-done = (f32[1,256,512]{2,1,0:T(8,128)}, f32[1,256,512]{2,1,0:T(8,128)}, f32[1,256,256]{2,1,0:T(8,128)}, f32[1,256,256]{2,1,0:T(8,128)}) async-done(((f32[1,256,512]{2,1,0:T(8,128)}, f32[1,256,512]{2,1,0:T(8,128)}, f32[1,256,256]{2,1,0:T(8,128)}, f32[1,256,256]{2,1,0:T(8,128)}), (f32[1,256,512]{2,1,0:T(8,128)}, f32[1,256,512]{2,1,0:T(8,128)}, f32[1,256,256]{2,1,0:T(8,128)}, ...) | async-done | bytes 1572880 | tf_op jit(solution)/shard_map/psum | solution.py:160
  452.7 1.9 broadcast_multiply_fusion.2
  454.6 2.3 broadcast_multiply_fusion
  (172 shorter events, 48.9 us)
Async XLA Ops:
  7.2 39.3 %copy-start = (bf16[4,512,256]{2,1,0:T(8,128)(2,1)S(1)}, bf16[4,512,256]{2,1,0:T(8,128)(2,1)}, u32[]{:S(2)}) copy-start(bf16[4,512,256]{2,1,0:T(8,128)(2,1)} %param.8) | copy-start | bytes 3145732
  7.2 40.3 %all-gather.5.cloned.1.call-start = ((), (), s32[]{:S(2)}) async-start(), calls=%async_computation.7 | async-start | bytes 1310720 | tf_op jit(solution)/shard_map/all_gather | solution.py:87
  7.9 60.6 %all-gather.3.cloned.1.call-start = ((), (), s32[]{:S(2)}) async-start(), calls=%async_computation.6 | async-start | bytes 1310720 | tf_op jit(solution)/shard_map/all_gather | solution.py:86
  8.7 187.8 %reduce-scatter.11.cloned.1.call-start = ((), (), s32[]{:S(2)}) async-start(), calls=%async_computation.11 | async-start | bytes 1310720 | tf_op jit(solution)/shard_map/reduce_scatter | solution.py:145
  9.7 39.1 %collective-permute-start = (bf16[1,512,256]{2,1,0:T(8,128)(2,1)S(1)}, bf16[1,512,256]{2,1,0:T(8,128)(2,1)S(1)}, u32[]{:S(2)}, u32[]{:S(2)}) collective-permute-start(bf16[1,512,256]{2,1,0:T(8,128)(2,1)S(1)} %constant_dynamic-slice_fusion), channel_id=1, source_target_pairs={{0,4},{1,5},{2,6},{3,7},{4,8},{5,9},{6,10},{7,11},{8,12},{9,13},{1... | collective-permute-start | bytes 786440 | tf_op jit(solution)/shard_map/ppermute | solution.py:13
  29.1 55.0 %copy-start.11 = (bf16[4,256,256]{2,1,0:T(8,128)(2,1)}, bf16[4,256,256]{2,1,0:T(8,128)(2,1)S(1)}, u32[]{:S(2)}) copy-start(bf16[4,256,256]{2,1,0:T(8,128)(2,1)S(1)} %all_gather.15) | copy-start | bytes 1572868
  48.8 19.7 %copy-start.14 = (bf16[1,512,256]{2,1,0:T(8,128)(2,1)}, bf16[1,512,256]{2,1,0:T(8,128)(2,1)S(1)}, u32[]{:S(2)}) copy-start(bf16[1,512,256]{2,1,0:T(8,128)(2,1)S(1)} %collective-permute-done) | copy-start | bytes 786436
  69.8 14.3 %copy-start.12 = (bf16[4,256,512]{2,1,0:T(8,128)(2,1)S(1)}, bf16[4,256,512]{2,1,0:T(8,128)(2,1)}, u32[]{:S(2)}) copy-start(bf16[4,256,512]{2,1,0:T(8,128)(2,1)} %all-gather.3.cloned.1.call-done) | copy-start | bytes 3145732
  70.5 13.6 %collective-permute-start.1 = (bf16[1,512,256]{2,1,0:T(8,128)(2,1)S(1)}, bf16[1,512,256]{2,1,0:T(8,128)(2,1)S(1)}, u32[]{:S(2)}, u32[]{:S(2)}) collective-permute-start(bf16[1,512,256]{2,1,0:T(8,128)(2,1)S(1)} %fusion.14), channel_id=1, source_target_pairs={{0,8},{1,9},{2,10},{3,11},{4,12},{5,13},{6,14},{7,15},{8,16},{9,17... | collective-permute-start | bytes 786440 | tf_op jit(solution)/shard_map/ppermute | solution.py:13
  86.3 8.8 %collective-permute-start.2 = (bf16[1,512,256]{2,1,0:T(8,128)(2,1)S(1)}, bf16[1,512,256]{2,1,0:T(8,128)(2,1)S(1)}, u32[]{:S(2)}, u32[]{:S(2)}) collective-permute-start(bf16[1,512,256]{2,1,0:T(8,128)(2,1)S(1)} %fusion.13), channel_id=1, source_target_pairs={{0,16},{1,17},{2,18},{3,19},{4,20},{5,21},{6,22},{7,23},{8,24},{9,... | collective-permute-start | bytes 786440 | tf_op jit(solution)/shard_map/ppermute | solution.py:13
  98.0 9.9 %collective-permute-start.3 = (bf16[1,512,256]{2,1,0:T(8,128)(2,1)S(1)}, bf16[1,512,256]{2,1,0:T(8,128)(2,1)S(1)}, u32[]{:S(2)}, u32[]{:S(2)}) collective-permute-start(bf16[1,512,256]{2,1,0:T(8,128)(2,1)S(1)} %fusion.12), channel_id=1, source_target_pairs={{0,32},{1,33},{2,34},{3,35},{4,36},{5,37},{6,38},{7,39},{8,40},{9,... | collective-permute-start | bytes 786440 | tf_op jit(solution)/shard_map/ppermute | solution.py:13
  109.8 10.1 %collective-permute-start.4 = (bf16[1,512,256]{2,1,0:T(8,128)(2,1)}, bf16[1,512,256]{2,1,0:T(8,128)(2,1)}, u32[]{:S(2)}, u32[]{:S(2)}) collective-permute-start(bf16[1,512,256]{2,1,0:T(8,128)(2,1)} %fusion.16), channel_id=1, source_target_pairs={{32,0},{33,1},{34,2},{35,3},{36,4},{37,5},{38,6},{39,7},{40,8},{41... | collective-permute-start | bytes 786440 | tf_op jit(solution)/shard_map/ppermute | solution.py:13
  112.5 84.0 %reduce-scatter.9.cloned.1.call-start = ((), (), s32[]{:S(2)}) async-start(), calls=%async_computation.10 | async-start | bytes 1310720 | tf_op jit(solution)/shard_map/reduce_scatter | solution.py:142
  123.9 8.4 %collective-permute-start.5 = (bf16[1,512,256]{2,1,0:T(8,128)(2,1)S(1)}, bf16[1,512,256]{2,1,0:T(8,128)(2,1)S(1)}, u32[]{:S(2)}, u32[]{:S(2)}) collective-permute-start(bf16[1,512,256]{2,1,0:T(8,128)(2,1)S(1)} %fusion.17), channel_id=1, source_target_pairs={{16,0},{17,1},{18,2},{19,3},{20,4},{21,5},{22,6},{23,7},{24,8},{25... | collective-permute-start | bytes 786440 | tf_op jit(solution)/shard_map/ppermute | solution.py:13
  134.5 12.2 %collective-permute-start.6 = (bf16[1,512,256]{2,1,0:T(8,128)(2,1)S(1)}, bf16[1,512,256]{2,1,0:T(8,128)(2,1)S(1)}, u32[]{:S(2)}, u32[]{:S(2)}) collective-permute-start(bf16[1,512,256]{2,1,0:T(8,128)(2,1)S(1)} %fusion.18), channel_id=1, source_target_pairs={{8,0},{9,1},{10,2},{11,3},{12,4},{13,5},{14,6},{15,7},{16,8},{17,9... | collective-permute-start | bytes 786440 | tf_op jit(solution)/shard_map/ppermute | solution.py:13
  149.0 74.4 %reduce-scatter.7.cloned.1.call-start = ((), (), s32[]{:S(2)}) async-start(), calls=%async_computation.9 | async-start | bytes 2621440 | tf_op jit(solution)/shard_map/reduce_scatter | solution.py:139
  155.6 102.8 %reduce-scatter.5.cloned.1.call-start = ((), (), s32[]{:S(2)}) async-start(), calls=%async_computation.8 | async-start | bytes 2621440 | tf_op jit(solution)/shard_map/reduce_scatter | solution.py:136
  164.5 24.8 %copy-start.44 = (bf16[1,512,256]{2,1,0:T(8,128)(2,1)S(1)}, bf16[1,512,256]{2,1,0:T(8,128)(2,1)}, u32[]{:S(2)}) copy-start(bf16[1,512,256]{2,1,0:T(8,128)(2,1)} %copy-done.42) | copy-start | bytes 786436
  164.5 27.2 %all-to-all-start = ((bf16[4,1,512,256]{3,2,1,0:T(8,128)(2,1)}), bf16[4,1,512,256]{3,2,1,0:T(8,128)(2,1)S(1)}, u32[]{:S(2)}, u32[]{:S(2)}) async-start(bf16[4,1,512,256]{3,2,1,0:T(8,128)(2,1)} %stack.82), calls=%async_computation | async-start | bytes 2097152 | tf_op jit(solution)/shard_map/all_to_all | solution.py:112
  169.7 20.9 %copy-start.39 = (bf16[1,512,256]{2,1,0:T(8,128)(2,1)S(1)}, bf16[1,512,256]{2,1,0:T(8,128)(2,1)}, u32[]{:S(2)}) copy-start(bf16[1,512,256]{2,1,0:T(8,128)(2,1)} %copy-done.38) | copy-start | bytes 786436
  169.7 20.9 %copy-start.41 = (bf16[1,512,256]{2,1,0:T(8,128)(2,1)S(1)}, bf16[1,512,256]{2,1,0:T(8,128)(2,1)}, u32[]{:S(2)}) copy-start(bf16[1,512,256]{2,1,0:T(8,128)(2,1)} %copy-done.40) | copy-start | bytes 786436
  171.1 18.2 %collective-permute-start.7 = (bf16[1,512,256]{2,1,0:T(8,128)(2,1)S(1)}, bf16[1,512,256]{2,1,0:T(8,128)(2,1)S(1)}, u32[]{:S(2)}, u32[]{:S(2)}) collective-permute-start(bf16[1,512,256]{2,1,0:T(8,128)(2,1)S(1)} %fusion.19), channel_id=1, source_target_pairs={{4,0},{5,1},{6,2},{7,3},{8,4},{9,5},{10,6},{11,7},{12,8},{13,9},{1... | collective-permute-start | bytes 786440 | tf_op jit(solution)/shard_map/ppermute | solution.py:13
  191.7 66.8 %all-to-all-start.1 = ((bf16[4,1,512,256]{3,2,1,0:T(8,128)(2,1)}), bf16[4,1,512,256]{3,2,1,0:T(8,128)(2,1)S(1)}, u32[]{:S(2)}, u32[]{:S(2)}) async-start(bf16[4,1,512,256]{3,2,1,0:T(8,128)(2,1)} %pad_maximum_fusion.2), calls=%async_computation.1 | async-start | bytes 2097152 | tf_op jit(solution)/shard_map/all_to_all | solution.py:134
  196.5 256.2 %all-reduce.3.cloned.1.call-start = ((), (), s32[]{:S(2)}) async-start(), calls=%async_computation.12 | async-start | bytes 3145728 | tf_op jit(solution)/shard_map/psum | solution.py:160
  (39 other events, 206.0 us)
Sparse Core Ops, SparseCore 0:
  9.8 30.3 all-gather.4
  42.0 26.4 all-gather.2
  112.6 31.7 reduce-scatter.10
  149.1 34.1 reduce-scatter.8
  185.7 37.6 reduce-scatter.6
  225.7 32.7 reduce-scatter.4
  262.1 190.5 all-reduce.2
